TPU v7x, 32 devices: a whole 2x2x4 slice. The times are simulated.
32 devices in a mesh: dp: 8 (over y, x, core), seq: 4 (over z).
Axes of the slice: x: 2, y: 2, z: 4, core: 2. Of those that a mesh axis runs over, the one named last changes fastest.
Arguments:
- inputs: bfloat16 [24, 1024, 768], P('dp', 'seq'), may hold values from -6 to 6
- segment_ids: int32 [24, 1024], P('dp', 'seq'), may hold values from 0 to 3, never falling along the last dimension, each value on 1 to 512 neighbouring positions
- norm1_gain: bfloat16 [768], P('dp'), may hold values from 0.5 to 1.5
- norm1_shift: bfloat16 [768], P('dp'), may hold values from -1.5 to 1.5
- query_weight: bfloat16 [768, 768], P('dp'), may hold values from -0.4375 to 0.4375
- query_bias: bfloat16 [768], P('dp'), may hold values from -2.5 to 2.5
- key_weight: bfloat16 [768, 768], P('dp'), may hold values from -0.21875 to 0.21875
- value_weight: bfloat16 [768, 768], P('dp'), may hold values from -0.21875 to 0.21875
- value_bias: bfloat16 [768], P('dp'), may hold values from -1.5 to 1.5
- out_weight: bfloat16 [768, 768], P('dp'), may hold values from -0.625 to 0.625
- out_bias: bfloat16 [768], P('dp'), may hold values from -1.5 to 1.5
- norm2_gain: bfloat16 [768], P('dp'), may hold values from 0.5 to 1.5
- norm2_shift: bfloat16 [768], P('dp'), may hold values from -1.5 to 1.5
- fc1_weight: bfloat16 [768, 3072], P('dp'), may hold values from -0.21875 to 0.21875
- fc1_bias: bfloat16 [3072], P('dp'), may hold values from -1.5 to 1.5
- fc2_weight: bfloat16 [3072, 768], P('dp'), may hold values from -0.15625 to 0.15625
- fc2_bias: bfloat16 [768], P('dp'), may hold values from -1.5 to 1.5
- grad_output: bfloat16 [24, 1024, 768], P('dp', 'seq'), may hold values from -6 to 6
Outputs:
- output: bfloat16 [24, 1024, 768], P('dp', 'seq')
- grad_inputs: bfloat16 [24, 1024, 768], P('dp', 'seq')
- grad_norm1_gain: float32 [768], P('dp')
- grad_norm1_shift: float32 [768], P('dp')
- grad_query_weight: float32 [768, 768], P('dp')
- grad_query_bias: float32 [768], P('dp')
- grad_key_weight: float32 [768, 768], P('dp')
- grad_value_weight: float32 [768, 768], P('dp')
- grad_value_bias: float32 [768], P('dp')
- grad_out_weight: float32 [768, 768], P('dp')
- grad_out_bias: float32 [768], P('dp')
- grad_norm2_gain: float32 [768], P('dp')
- grad_norm2_shift: float32 [768], P('dp')
- grad_fc1_weight: float32 [768, 3072], P('dp')
- grad_fc1_bias: float32 [3072], P('dp')
- grad_fc2_weight: float32 [3072, 768], P('dp')
- grad_fc2_bias: float32 [768], P('dp')
Inputs may be any that keep to these rules, and one draw needn't show every extreme that they name: `segment_ids`: within each sequence, segment numbers never fall along the positions; each segment is a run of 1 to 512 positions.
All inputs are finite; a program needn't handle non-finite values.
Results may differ from a plain program's by a relative error of at most 0.017.
Values may be sent and summed in bfloat16 or wider, within the bound.
No kernel may reach another device: no remote copies, remote signals or barrier semaphores. Data moves between devices by JAX's collectives and lax.ppermute only.
A program may use at most 192 MiB of HBM per device.

v0:
```python
import jax
import jax.numpy as jnp
from jax import lax
from jax.sharding import PartitionSpec as P

HD = 64
EPSILON = 1e-05


def layer_norm(values, gain, shift):
    center = values - jnp.mean(values, axis=-1, keepdims=True)
    inverse = lax.rsqrt(jnp.mean(center * center, axis=-1, keepdims=True) + EPSILON)
    normed = center * inverse
    return (normed * gain + shift, normed, inverse)


def norm_back(grad, normed, inverse, gain):
    scaled = grad * gain
    return inverse * (
        scaled
        - jnp.mean(scaled, axis=-1, keepdims=True)
        - normed * jnp.mean(scaled * normed, axis=-1, keepdims=True)
    )


def gelu_slope(pre_act):
    return (
        0.5 * (1.0 + lax.erf(pre_act * 0.7071067811865476))
        + pre_act * jnp.exp(-0.5 * pre_act * pre_act) * 0.3989422804014327
    )


def cross_rows(left, right):
    return lax.dot_general(
        left, right, (((0,), (0,)), ((), ())), preferred_element_type=jnp.float32
    )


def times_transpose(left, right):
    return lax.dot_general(
        left, right, (((1,), (1,)), ((), ())), preferred_element_type=jnp.float32
    )


def to_pairs(array, heads_here):
    seqs_here, positions, _ = array.shape
    shaped = array.reshape(seqs_here, positions, heads_here, HD).transpose(0, 2, 1, 3)
    return shaped.reshape(seqs_here * heads_here, positions, HD)


def from_pairs(array, seqs_here, heads_here):
    positions = array.shape[1]
    shaped = array.reshape(seqs_here, heads_here, positions, HD).transpose(0, 2, 1, 3)
    return shaped.reshape(seqs_here, positions, heads_here * HD)


def masked_scores(query_pair, key_pair, segment_row):
    scores = jnp.einsum(
        "qd,kd->qk", query_pair, key_pair, preferred_element_type=jnp.float32
    ) * HD ** (-0.5)
    same_segment = segment_row[:, None] == segment_row[None, :]
    return jnp.where(same_segment, scores, -1e30)


def attend_forward(packed):
    query_pair, key_pair, value_pair, segment_row = packed
    scores = masked_scores(query_pair, key_pair, segment_row)
    highest = jnp.max(scores, axis=-1, keepdims=True)
    expon = jnp.exp(scores - highest)
    totals = jnp.sum(expon, axis=-1, keepdims=True)
    probs = (expon / totals).astype(jnp.bfloat16)
    result = jnp.dot(probs, value_pair, preferred_element_type=jnp.float32).astype(jnp.bfloat16)
    return (result, (highest + jnp.log(totals))[:, 0])


def attend_backward(packed):
    query_pair, key_pair, value_pair, segment_row, logsum, grad_pair = packed
    scores = masked_scores(query_pair, key_pair, segment_row)
    probs = jnp.exp(scores - logsum[:, None])
    grad_probs = jnp.einsum("qd,kd->qk", grad_pair, value_pair, preferred_element_type=jnp.float32)
    delta = jnp.sum(probs * grad_probs, axis=-1, keepdims=True)
    grad_scores = (probs * (grad_probs - delta)).astype(jnp.bfloat16)
    factor = HD ** (-0.5)
    grad_query = (
        jnp.einsum("qk,kd->qd", grad_scores, key_pair, preferred_element_type=jnp.float32) * factor
    ).astype(jnp.bfloat16)
    grad_key = (
        jnp.einsum("qk,qd->kd", grad_scores, query_pair, preferred_element_type=jnp.float32)
        * factor
    ).astype(jnp.bfloat16)
    grad_value = jnp.einsum(
        "qk,qd->kd", probs.astype(jnp.bfloat16), grad_pair, preferred_element_type=jnp.float32
    ).astype(jnp.bfloat16)
    return (grad_query, grad_key, grad_value)


def column_sum(array):
    return jnp.sum(array.astype(jnp.float32), axis=0)


def per_device(
    inputs,
    segment_ids,
    norm1_gain,
    norm1_shift,
    query_weight,
    query_bias,
    key_weight,
    value_weight,
    value_bias,
    out_weight,
    out_bias,
    norm2_gain,
    norm2_shift,
    fc1_weight,
    fc1_bias,
    fc2_weight,
    fc2_bias,
    grad_output,
):
    seqs_here, positions, model_width = inputs.shape
    token_rows = seqs_here * positions
    (
        first_gain,
        first_shift,
        w_query,
        b_query,
        w_key,
        w_value,
        b_value,
        w_out,
        b_out,
        second_gain,
        second_shift,
        w_up,
        b_up,
        w_down,
        b_down,
    ) = (
        lax.all_gather(norm1_gain, "dp", axis=0, tiled=True),
        lax.all_gather(norm1_shift, "dp", axis=0, tiled=True),
        lax.all_gather(query_weight, "dp", axis=0, tiled=True),
        lax.all_gather(query_bias, "dp", axis=0, tiled=True),
        lax.all_gather(key_weight, "dp", axis=0, tiled=True),
        lax.all_gather(value_weight, "dp", axis=0, tiled=True),
        lax.all_gather(value_bias, "dp", axis=0, tiled=True),
        lax.all_gather(out_weight, "dp", axis=0, tiled=True),
        lax.all_gather(out_bias, "dp", axis=0, tiled=True),
        lax.all_gather(norm2_gain, "dp", axis=0, tiled=True),
        lax.all_gather(norm2_shift, "dp", axis=0, tiled=True),
        lax.all_gather(fc1_weight, "dp", axis=0, tiled=True),
        lax.all_gather(fc1_bias, "dp", axis=0, tiled=True),
        lax.all_gather(fc2_weight, "dp", axis=0, tiled=True),
        lax.all_gather(fc2_bias, "dp", axis=0, tiled=True),
    )
    full_segments = lax.all_gather(segment_ids, "seq", axis=1, tiled=True)
    flat_in = inputs.reshape(token_rows, model_width).astype(jnp.float32)
    normed_one, unit_one, inverse_one = layer_norm(
        flat_in, first_gain.astype(jnp.float32), first_shift.astype(jnp.float32)
    )
    act_one = normed_one.astype(jnp.bfloat16)
    query_tok = (
        jnp.dot(act_one, w_query, preferred_element_type=jnp.float32) + b_query.astype(jnp.float32)
    ).astype(jnp.bfloat16)
    key_tok = jnp.dot(act_one, w_key, preferred_element_type=jnp.float32).astype(jnp.bfloat16)
    value_tok = (
        jnp.dot(act_one, w_value, preferred_element_type=jnp.float32) + b_value.astype(jnp.float32)
    ).astype(jnp.bfloat16)
    query_heads, key_heads, value_heads = (
        lax.all_to_all(
            query_tok.reshape(seqs_here, positions, model_width),
            "seq",
            split_axis=2,
            concat_axis=1,
            tiled=True,
        ),
        lax.all_to_all(
            key_tok.reshape(seqs_here, positions, model_width),
            "seq",
            split_axis=2,
            concat_axis=1,
            tiled=True,
        ),
        lax.all_to_all(
            value_tok.reshape(seqs_here, positions, model_width),
            "seq",
            split_axis=2,
            concat_axis=1,
            tiled=True,
        ),
    )
    heads_here = query_heads.shape[2] // HD
    query_pairs = to_pairs(query_heads, heads_here)
    key_pairs = to_pairs(key_heads, heads_here)
    value_pairs = to_pairs(value_heads, heads_here)
    segment_pairs = jnp.repeat(full_segments, heads_here, axis=0)
    attn_pairs, logsum = lax.map(
        attend_forward, (query_pairs, key_pairs, value_pairs, segment_pairs)
    )
    attn_heads = from_pairs(attn_pairs, seqs_here, heads_here)
    attn_tok = lax.all_to_all(attn_heads, "seq", split_axis=1, concat_axis=2, tiled=True).reshape(
        token_rows, model_width
    )
    middle = (
        flat_in
        + jnp.dot(attn_tok, w_out, preferred_element_type=jnp.float32)
        + b_out.astype(jnp.float32)
    )
    normed_two, unit_two, inverse_two = layer_norm(
        middle, second_gain.astype(jnp.float32), second_shift.astype(jnp.float32)
    )
    act_two = normed_two.astype(jnp.bfloat16)
    pre_act = jnp.dot(act_two, w_up, preferred_element_type=jnp.float32) + b_up.astype(jnp.float32)
    hidden = jax.nn.gelu(pre_act, approximate=False).astype(jnp.bfloat16)
    result = (
        middle
        + jnp.dot(hidden, w_down, preferred_element_type=jnp.float32)
        + b_down.astype(jnp.float32)
    )
    output = result.astype(jnp.bfloat16).reshape(seqs_here, positions, model_width)
    first_gain_b, w_query_b, w_key_b, w_value_b, w_out_b, second_gain_b, w_up_b, w_down_b = (
        lax.all_gather(norm1_gain, "dp", axis=0, tiled=True),
        lax.all_gather(query_weight, "dp", axis=0, tiled=True),
        lax.all_gather(key_weight, "dp", axis=0, tiled=True),
        lax.all_gather(value_weight, "dp", axis=0, tiled=True),
        lax.all_gather(out_weight, "dp", axis=0, tiled=True),
        lax.all_gather(norm2_gain, "dp", axis=0, tiled=True),
        lax.all_gather(fc1_weight, "dp", axis=0, tiled=True),
        lax.all_gather(fc2_weight, "dp", axis=0, tiled=True),
    )
    grad_down = grad_output.reshape(token_rows, model_width)
    d_b_down = column_sum(grad_down)
    d_w_down = cross_rows(hidden, grad_down)
    grad_hidden = times_transpose(grad_down, w_down_b)
    grad_pre = (grad_hidden * gelu_slope(pre_act)).astype(jnp.bfloat16)
    d_b_up = column_sum(grad_pre)
    d_w_up = cross_rows(act_two, grad_pre)
    grad_two = times_transpose(grad_pre, w_up_b)
    d_second_gain = jnp.sum(grad_two * unit_two, axis=0)
    d_second_shift = jnp.sum(grad_two, axis=0)
    grad_middle = grad_down.astype(jnp.float32) + norm_back(
        grad_two, unit_two, inverse_two, second_gain_b.astype(jnp.float32)
    )
    grad_branch = grad_middle.astype(jnp.bfloat16)
    d_b_out = column_sum(grad_branch)
    d_w_out = cross_rows(attn_tok, grad_branch)
    grad_attn = (
        times_transpose(grad_branch, w_out_b)
        .astype(jnp.bfloat16)
        .reshape(seqs_here, positions, model_width)
    )
    grad_attn_heads = lax.all_to_all(grad_attn, "seq", split_axis=2, concat_axis=1, tiled=True)
    grad_query_pairs, grad_key_pairs, grad_value_pairs = lax.map(
        attend_backward,
        (
            query_pairs,
            key_pairs,
            value_pairs,
            segment_pairs,
            logsum,
            to_pairs(grad_attn_heads, heads_here),
        ),
    )
    grad_query_tok, grad_key_tok, grad_value_tok = (
        lax.all_to_all(
            from_pairs(grad_query_pairs, seqs_here, heads_here),
            "seq",
            split_axis=1,
            concat_axis=2,
            tiled=True,
        ),
        lax.all_to_all(
            from_pairs(grad_key_pairs, seqs_here, heads_here),
            "seq",
            split_axis=1,
            concat_axis=2,
            tiled=True,
        ),
        lax.all_to_all(
            from_pairs(grad_value_pairs, seqs_here, heads_here),
            "seq",
            split_axis=1,
            concat_axis=2,
            tiled=True,
        ),
    )
    grad_query_tok = grad_query_tok.reshape(token_rows, model_width)
    grad_key_tok = grad_key_tok.reshape(token_rows, model_width)
    grad_value_tok = grad_value_tok.reshape(token_rows, model_width)
    d_b_query = column_sum(grad_query_tok)
    d_b_value = column_sum(grad_value_tok)
    d_w_query = cross_rows(act_one, grad_query_tok)
    d_w_key = cross_rows(act_one, grad_key_tok)
    d_w_value = cross_rows(act_one, grad_value_tok)
    grad_one = (
        times_transpose(grad_query_tok, w_query_b)
        + times_transpose(grad_key_tok, w_key_b)
        + times_transpose(grad_value_tok, w_value_b)
    )
    d_first_gain = jnp.sum(grad_one * unit_one, axis=0)
    d_first_shift = jnp.sum(grad_one, axis=0)
    grad_inputs = grad_middle + norm_back(
        grad_one, unit_one, inverse_one, first_gain_b.astype(jnp.float32)
    )
    grad_inputs = grad_inputs.astype(jnp.bfloat16).reshape(seqs_here, positions, model_width)
    (
        part_first_gain,
        part_first_shift,
        part_w_query,
        part_b_query,
        part_w_key,
        part_w_value,
        part_b_value,
        part_w_out,
        part_b_out,
        part_second_gain,
        part_second_shift,
        part_w_up,
        part_b_up,
        part_w_down,
        part_b_down,
    ) = (
        lax.psum_scatter(d_first_gain, "dp", scatter_dimension=0, tiled=True),
        lax.psum_scatter(d_first_shift, "dp", scatter_dimension=0, tiled=True),
        lax.psum_scatter(d_w_query, "dp", scatter_dimension=0, tiled=True),
        lax.psum_scatter(d_b_query, "dp", scatter_dimension=0, tiled=True),
        lax.psum_scatter(d_w_key, "dp", scatter_dimension=0, tiled=True),
        lax.psum_scatter(d_w_value, "dp", scatter_dimension=0, tiled=True),
        lax.psum_scatter(d_b_value, "dp", scatter_dimension=0, tiled=True),
        lax.psum_scatter(d_w_out, "dp", scatter_dimension=0, tiled=True),
        lax.psum_scatter(d_b_out, "dp", scatter_dimension=0, tiled=True),
        lax.psum_scatter(d_second_gain, "dp", scatter_dimension=0, tiled=True),
        lax.psum_scatter(d_second_shift, "dp", scatter_dimension=0, tiled=True),
        lax.psum_scatter(d_w_up, "dp", scatter_dimension=0, tiled=True),
        lax.psum_scatter(d_b_up, "dp", scatter_dimension=0, tiled=True),
        lax.psum_scatter(d_w_down, "dp", scatter_dimension=0, tiled=True),
        lax.psum_scatter(d_b_down, "dp", scatter_dimension=0, tiled=True),
    )
    (
        shard_first_gain,
        shard_first_shift,
        shard_w_query,
        shard_b_query,
        shard_w_key,
        shard_w_value,
        shard_b_value,
        shard_w_out,
        shard_b_out,
        shard_second_gain,
        shard_second_shift,
        shard_w_up,
        shard_b_up,
        shard_w_down,
        shard_b_down,
    ) = (
        lax.psum(part_first_gain.astype(jnp.bfloat16), "seq").astype(jnp.float32),
        lax.psum(part_first_shift.astype(jnp.bfloat16), "seq").astype(jnp.float32),
        lax.psum(part_w_query.astype(jnp.bfloat16), "seq").astype(jnp.float32),
        lax.psum(part_b_query.astype(jnp.bfloat16), "seq").astype(jnp.float32),
        lax.psum(part_w_key.astype(jnp.bfloat16), "seq").astype(jnp.float32),
        lax.psum(part_w_value.astype(jnp.bfloat16), "seq").astype(jnp.float32),
        lax.psum(part_b_value.astype(jnp.bfloat16), "seq").astype(jnp.float32),
        lax.psum(part_w_out.astype(jnp.bfloat16), "seq").astype(jnp.float32),
        lax.psum(part_b_out.astype(jnp.bfloat16), "seq").astype(jnp.float32),
        lax.psum(part_second_gain.astype(jnp.bfloat16), "seq").astype(jnp.float32),
        lax.psum(part_second_shift.astype(jnp.bfloat16), "seq").astype(jnp.float32),
        lax.psum(part_w_up.astype(jnp.bfloat16), "seq").astype(jnp.float32),
        lax.psum(part_b_up.astype(jnp.bfloat16), "seq").astype(jnp.float32),
        lax.psum(part_w_down.astype(jnp.bfloat16), "seq").astype(jnp.float32),
        lax.psum(part_b_down.astype(jnp.bfloat16), "seq").astype(jnp.float32),
    )
    return (
        output,
        grad_inputs,
        shard_first_gain,
        shard_first_shift,
        shard_w_query,
        shard_b_query,
        shard_w_key,
        shard_w_value,
        shard_b_value,
        shard_w_out,
        shard_b_out,
        shard_second_gain,
        shard_second_shift,
        shard_w_up,
        shard_b_up,
        shard_w_down,
        shard_b_down,
    )


def solution(mesh):
    placed = (
        P("dp", "seq", None),
        P("dp", "seq"),
        P("dp"),
        P("dp"),
        P("dp", None),
        P("dp"),
        P("dp", None),
        P("dp", None),
        P("dp"),
        P("dp", None),
        P("dp"),
        P("dp"),
        P("dp"),
        P("dp", None),
        P("dp"),
        P("dp", None),
        P("dp"),
        P("dp", "seq", None),
    )
    return jax.shard_map(
        per_device,
        mesh=mesh,
        in_specs=placed,
        out_specs=(
            P("dp", "seq", None),
            P("dp", "seq", None),
            P("dp"),
            P("dp"),
            P("dp", None),
            P("dp"),
            P("dp", None),
            P("dp", None),
            P("dp"),
            P("dp", None),
            P("dp"),
            P("dp"),
            P("dp"),
            P("dp", None),
            P("dp"),
            P("dp", None),
            P("dp"),
        ),
        check_vma=False,
    )
```

profile of v0, /device:TPU:0, one launch (start us, length us, event | category | flops | bytes accessed | tf_op | source)
XLA Modules:
  0.0 1093.1 jit_solution(9284306337476619404)
XLA Ops:
  15.2 26.3 %all-reduce.18 = (bf16[768]{0:T(1024)(128)(2,1)S(1)}, bf16[768]{0:T(1024)(128)(2,1)S(1)}, bf16[768]{0:T(1024)(128)(2,1)S(1)}, bf16[768]{0:T(1024)(128)(2,1)S(1)}...) all-reduce(bf16[768]{0:T(1024)(128)(2,1)S(1)} %dynamic-update-slice, ...), channel_id=1, replica_groups=mesh['dp'=8,'seq'=4] {'dp'}, use_global_device_ids=true, to_apply=%add.1 | all-reduce | flops 6144 | bytes 24576
  47.7 5.0 all-to-all-start
  53.4 9.6 all-gather.12.cloned.1.call-done
  70.2 16.2 %all-to-all-done = bf16[3,256,768]{1,0,2:T(4,128)(2,1)S(1)} async-done(((bf16[3,256,768]{1,0,2:T(4,128)(2,1)}), bf16[3,256,768]{1,0,2:T(4,128)(2,1)S(1)}, u32[]{:S(2)}, u32[]{:S(2)}) %all-to-all-start) | async-done | bytes 1179680 | tf_op jit(solution)/shard_map/all_to_all | solution.py:170
  86.5 4.3 all-to-all-start.2
  98.7 28.6 %all-to-all-done.2 = bf16[3,256,768]{1,0,2:T(4,128)(2,1)} async-done(((bf16[3,256,768]{1,0,2:T(4,128)(2,1)}), bf16[3,256,768]{1,0,2:T(4,128)(2,1)}, u32[]{:S(2)}, u32[]{:S(2)}) %all-to-all-start.2) | async-done | bytes 1179680 | tf_op jit(solution)/shard_map/all_to_all | solution.py:184
  127.3 4.3 all-to-all-start.1
  132.3 41.2 %all_gather.56 = s32[3,1024]{1,0:T(4,128)S(1)} all-gather(s32[3,256]{1,0:T(4,128)S(1)} %copy-done.26), channel_id=1, replica_groups=mesh['dp'=8,'seq'=4] {'seq'}, dimensions={1}, use_global_device_ids=true | all-gather | bytes 15360 | tf_op jit(solution)/shard_map/all_gather | solution.py:156
  202.1 99.2 %while.26 = (s32[]{:T(128)}, bf16[9,1024,64]{1,2,0:T(8,128)(2,1)}, f32[9,1024]{1,0:T(8,128)}, s32[9,1024]{1,0:T(8,128)}, bf16[9,1024,64]{2,1,0:T(8,128)(2,1)S(1)...) while((s32[]{:T(128)}, bf16[9,1024,64]{1,2,0:T(8,128)(2,1)}, ...), condition=%wide.region_5.6_spmd, body=%wide.region_2.5_spmd.sunk | while | flops 284228608 | bytes 30349440 | solution.py:197
  208.9 4.2 fusion.156
  219.9 4.2 fusion.156
  231.0 4.2 fusion.156
  242.0 4.2 fusion.156
  253.0 4.2 fusion.156
  264.0 4.2 fusion.156
  275.0 4.2 fusion.156
  286.0 4.2 fusion.156
  297.1 4.2 fusion.156
  301.3 4.2 copy.112
  305.5 4.6 all-to-all-start.3
  311.4 10.1 all-gather
  322.1 33.6 %all-to-all-done.3 = bf16[3,1024,192]{2,0,1:T(4,128)(2,1)} async-done(((bf16[3,1024,192]{2,0,1:T(4,128)(2,1)}), bf16[3,1024,192]{2,0,1:T(4,128)(2,1)}, u32[]{:S(2)}, u32[]{:S(2)}) %all-to-all-start.3) | async-done | bytes 1179680 | tf_op jit(solution)/shard_map/all_to_all | solution.py:201
  364.3 27.2 %fusion.56 = (bf16[768,3072]{1,0:T(8,128)(2,1)}, f32[768,3072]{1,0:T(8,128)}) fusion(f32[3072]{0:T(1024)} %bitcast.275, bf16[768,3072]{1,0:T(8,128)(2,1)} %all-gather.16.cloned.1.call-done, f32[768,768]{1,0:T(8,128)S(1)} %get-tuple-element.265, f32[768]{0:T(1024)S(1)} %convert_element_type.227, f32[768]{0:T(1024)S(1)} %convert_element_type.226, ...), kind=kOutput, calls=%fused_computation.64 | convolution fusion | flops 3782541312 | bytes 21258240 | tf_op jit(solution)/shard_map/dot_general | solution.py:213
  391.5 11.6 %convert_reduce_fusion = (f32[3072]{0:T(1024)}, bf16[768,3072]{1,0:T(8,128)(2,1)S(1)}) fusion(f32[768,3072]{1,0:T(8,128)} %get-tuple-element.267, f32[3072]{0:T(1024)} %bitcast.276, bf16[768,768]{1,0:T(8,128)(2,1)} %bitcast.249, bf16[3072,768]{1,0:T(8,128)(2,1)} %all-gather.18.cloned.1.call-done), kind=kOutput, calls=%fused_computation.71 | convolution fusion | flops 3654546432 | bytes 20078592 | tf_op jit(solution)/shard_map/dot_general | solution.py:40
  403.2 4.8 multiply_reduce_fusion.1
  415.4 4.3 all-to-all-start.4
  419.8 4.5 fusion.90
  424.4 31.9 %all-to-all-done.4 = bf16[3,256,768]{1,0,2:T(4,128)(2,1)} async-done(((bf16[3,256,768]{1,0,2:T(4,128)(2,1)}), bf16[3,256,768]{1,0,2:T(4,128)(2,1)}, u32[]{:S(2)}, u32[]{:S(2)}) %all-to-all-start.4) | async-done | bytes 1179680 | tf_op jit(solution)/shard_map/all_to_all | solution.py:252
  467.1 124.2 %while.27 = (s32[]{:T(128)}, bf16[9,1024,64]{1,2,0:T(8,128)(2,1)}, bf16[9,1024,64]{1,2,0:T(8,128)(2,1)}, bf16[9,1024,64]{1,2,0:T(8,128)(2,1)}, s32[9,1024]{1,0:T...) while((s32[]{:T(128)}, bf16[9,1024,64]{1,2,0:T(8,128)(2,1)}, ...), condition=%wide.region_12.13_spmd, body=%wide.region_10.12_spmd.sunk | while | flops 681901056 | bytes 33465460 | solution.py:253
  595.3 4.4 all-to-all-start.5
  602.0 45.4 %all-to-all-done.5 = bf16[3,1024,192]{2,0,1:T(4,128)(2,1)} async-done(((bf16[3,1024,192]{2,0,1:T(4,128)(2,1)}), bf16[3,1024,192]{2,0,1:T(4,128)(2,1)}, u32[]{:S(2)}, u32[]{:S(2)}) %all-to-all-start.5) | async-done | bytes 1179680 | tf_op jit(solution)/shard_map/all_to_all | solution.py:265
  647.5 4.2 copy.124
  655.7 4.2 fusion.99
  660.0 4.1 copy.125
  664.0 51.4 %all_to_all.120 = bf16[3,1024,192]{2,0,1:T(4,128)(2,1)S(1)} all-to-all(bf16[3,1024,192]{2,0,1:T(4,128)(2,1)} %copy.125), channel_id=1, replica_groups=mesh['dp'=8,'seq'=4] {'seq'}, dimensions={1} | all-to-all | bytes 2359296 | tf_op jit(solution)/shard_map/all_to_all | solution.py:272
  722.1 4.2 fusion.100
  730.5 50.8 %all_to_all.121 = bf16[3,1024,192]{2,0,1:T(4,128)(2,1)S(1)} all-to-all(bf16[3,1024,192]{2,0,1:T(4,128)(2,1)} %copy.128), channel_id=1, replica_groups=mesh['dp'=8,'seq'=4] {'seq'}, dimensions={1} | all-to-all | bytes 2359296 | tf_op jit(solution)/shard_map/all_to_all | solution.py:279
  789.3 4.1 fusion.101
  793.5 9.0 fusion.93
  802.6 10.6 fusion.102
  817.2 8.6 add_convert_fusion
  825.8 4.4 copy.135
  839.9 4.1 fusion.97
  849.0 67.9 %reduce-scatter.15.cloned.1.call-done = f32[96,3072]{1,0:T(8,128)} async-done(((f32[768,3072]{1,0:T(8,128)}), f32[96,3072]{1,0:T(8,128)}) %reduce-scatter.15.cloned.1.call-update) | async-done | bytes 1179664 | tf_op jit(solution)/shard_map/reduce_scatter | solution.py:334
  919.0 77.7 %reduce-scatter.17.cloned.1.call-done = f32[384,768]{1,0:T(8,128)} async-done(((f32[3072,768]{1,0:T(8,128)}), f32[384,768]{1,0:T(8,128)}) %reduce-scatter.17.cloned.1.call-update) | async-done | bytes 1179664 | tf_op jit(solution)/shard_map/reduce_scatter | solution.py:336
  1005.2 26.3 %all-reduce.17 = (bf16[768]{0:T(1024)(128)(2,1)}, bf16[768]{0:T(1024)(128)(2,1)}, bf16[768]{0:T(1024)(128)(2,1)}, bf16[768]{0:T(1024)(128)(2,1)}, bf16[768]{0:T(...) all-reduce(f32[768]{0:T(1024)} %get-tuple-element.184, ...), channel_id=2, replica_groups=mesh['dp'=8,'seq'=4] {'dp'}, use_global_device_ids=true, to_apply=%region_16.17.clone | all-reduce | flops 9216 | bytes 55296
  1042.2 13.1 %all-reduce.19 = (bf16[96]{0:T(256)(128)(2,1)}, bf16[96]{0:T(256)(128)(2,1)}, bf16[96]{0:T(256)(128)(2,1)}, bf16[96]{0:T(256)(128)(2,1)}, bf16[96]{0:T(256)(128)...) all-reduce(bf16[96]{0:T(256)(128)(2,1)} %dynamic-slice.43, ...), channel_id=1, replica_groups=mesh['dp'=8,'seq'=4] {'seq'}, use_global_device_ids=true, to_apply=%region_17.18 | all-reduce | flops 1152 | bytes 4608 | tf_op jit(solution)/shard_map/psum | solution.py:356
  1070.8 8.2 all-reduce.23.cloned.1.call-done
  (382 shorter events, 362.9 us)
Async XLA Ops:
  7.2 4.9 copy-start.31
  7.2 34.9 %copy-start.1 = (bf16[3,256,768]{2,1,0:T(8,128)(2,1)S(1)}, bf16[3,256,768]{2,1,0:T(8,128)(2,1)}, u32[]{:S(2)}) copy-start(bf16[3,256,768]{2,1,0:T(8,128)(2,1)} %param.22) | copy-start | bytes 3538948
  7.2 6.1 copy-start.36
  7.2 6.4 copy-start.37
  7.2 6.6 copy-start.38
  7.2 6.8 copy-start.39
  7.3 7.0 copy-start.40
  7.3 7.3 copy-start.41
  7.3 7.5 copy-start.42
  7.3 7.7 copy-start.43
  7.3 35.4 %all-gather.8.cloned.1.call-start = ((), (), s32[]{:S(2)}) async-start(), calls=%async_computation.14 | async-start | bytes 1327104 | tf_op jit(solution)/shard_map/all_gather | solution.py:142
  8.0 54.9 %all-gather.12.cloned.1.call-start = ((), (), s32[]{:S(2)}) async-start(), calls=%async_computation.16 | async-start | bytes 1327104 | tf_op jit(solution)/shard_map/all_gather | solution.py:145
  10.3 31.3 %copy-start.18 = (f32[3,256]{1,0:T(4,128)}, f32[3,256]{1,0:T(4,128)S(1)}, u32[]{:S(2)}) copy-start(f32[3,256]{1,0:T(4,128)S(1)} %broadcast_multiply_fusion.5) | copy-start | bytes 9220
  12.1 30.6 %copy-start.19 = (f32[768]{0:T(1024)}, f32[768]{0:T(1024)S(1)}, u32[]{:S(2)}) copy-start(f32[768]{0:T(1024)S(1)} %div.35) | copy-start | bytes 9220
  47.7 38.8 %all-to-all-start = ((bf16[3,256,768]{1,0,2:T(4,128)(2,1)}), bf16[3,256,768]{1,0,2:T(4,128)(2,1)S(1)}, u32[]{:S(2)}, u32[]{:S(2)}) async-start(bf16[3,256,768]{1,0,2:T(4,128)(2,1)} %copy.100), calls=%async_computation | async-start | bytes 3145728 | tf_op jit(solution)/shard_map/all_to_all | solution.py:170
  52.6 38.8 %all-gather.10.cloned.1.call-start = ((), (), s32[]{:S(2)}) async-start(), calls=%async_computation.15 | async-start | bytes 1327104 | tf_op jit(solution)/shard_map/all_gather | solution.py:144
  86.5 40.9 %all-to-all-start.2 = ((bf16[3,256,768]{1,0,2:T(4,128)(2,1)}), bf16[3,256,768]{1,0,2:T(4,128)(2,1)}, u32[]{:S(2)}, u32[]{:S(2)}) async-start(bf16[3,256,768]{1,0,2:T(4,128)(2,1)} %copy.106), calls=%async_computation.2 | async-start | bytes 3145728 | tf_op jit(solution)/shard_map/all_to_all | solution.py:184
  90.8 270.2 %all-gather.14.cloned.1.call-start = ((), (), s32[]{:S(2)}) async-start(), calls=%async_computation.17 | async-start | bytes 1327104 | tf_op jit(solution)/shard_map/all_gather | solution.py:147
  98.7 33.6 %copy-start.26 = (s32[3,256]{1,0:T(4,128)S(1)}, s32[3,256]{1,0:T(4,128)}, u32[]{:S(2)}) copy-start(s32[3,256]{1,0:T(4,128)} %param.23) | copy-start | bytes 9220
  127.3 63.0 %all-to-all-start.1 = ((bf16[3,256,768]{1,0,2:T(4,128)(2,1)}), bf16[3,256,768]{1,0,2:T(4,128)(2,1)}, u32[]{:S(2)}, u32[]{:S(2)}) async-start(bf16[3,256,768]{1,0,2:T(4,128)(2,1)} %copy.103), calls=%async_computation.1 | async-start | bytes 3145728 | tf_op jit(solution)/shard_map/all_to_all | solution.py:177
  131.7 232.6 %all-gather.16.cloned.1.call-start = ((), (), s32[]{:S(2)}) async-start(), calls=%async_computation.18 | async-start | bytes 5308416 | tf_op jit(solution)/shard_map/all_gather | solution.py:151
  301.3 4.3 copy-start.4
  305.5 5.2 copy-start.30
  305.5 5.2 copy-start.29
  305.5 5.2 copy-start.28
  305.5 50.2 %all-to-all-start.3 = ((bf16[3,1024,192]{2,0,1:T(4,128)(2,1)}), bf16[3,1024,192]{2,0,1:T(4,128)(2,1)}, u32[]{:S(2)}, u32[]{:S(2)}) async-start(bf16[3,1024,192]{2,0,1:T(4,128)(2,1)} %copy.112), calls=%async_computation.3 | async-start | bytes 4194304 | tf_op jit(solution)/shard_map/all_to_all | solution.py:201
  310.1 81.4 %all-gather.18.cloned.1.call-start = ((), (), s32[]{:S(2)}) async-start(), calls=%async_computation.19 | async-start | bytes 5308416 | tf_op jit(solution)/shard_map/all_gather | solution.py:153
  391.5 11.6 %copy-start.32 = (bf16[768,3072]{1,0:T(8,128)(2,1)S(1)}, bf16[768,3072]{1,0:T(8,128)(2,1)}, u32[]{:S(2)}) copy-start(bf16[768,3072]{1,0:T(8,128)(2,1)} %all-gather.16.cloned.1.call-done) | copy-start | bytes 14155780
  403.2 4.8 copy-start.8
  403.2 4.8 copy-start.7
  415.4 40.9 %all-to-all-start.4 = ((bf16[3,256,768]{1,0,2:T(4,128)(2,1)}), bf16[3,256,768]{1,0,2:T(4,128)(2,1)}, u32[]{:S(2)}, u32[]{:S(2)}) async-start(bf16[3,256,768]{1,0,2:T(4,128)(2,1)} %copy.115), calls=%async_computation.4 | async-start | bytes 3145728 | tf_op jit(solution)/shard_map/all_to_all | solution.py:252
  419.8 418.5 %reduce-scatter.13.cloned.1.call-start = ((), (), s32[]{:S(2)}) async-start(), calls=%async_computation.23 | async-start | bytes 2654208 | tf_op jit(solution)/shard_map/reduce_scatter | solution.py:330
  595.3 52.1 %all-to-all-start.5 = ((bf16[3,1024,192]{2,0,1:T(4,128)(2,1)}), bf16[3,1024,192]{2,0,1:T(4,128)(2,1)}, u32[]{:S(2)}, u32[]{:S(2)}) async-start(bf16[3,1024,192]{2,0,1:T(4,128)(2,1)} %copy.122), calls=%async_computation.5 | async-start | bytes 4194304 | tf_op jit(solution)/shard_map/all_to_all | solution.py:265
  599.8 244.3 %reduce-scatter.7.cloned.1.call-start = ((), (), s32[]{:S(2)}) async-start(), calls=%async_computation.20 | async-start | bytes 2654208 | tf_op jit(solution)/shard_map/reduce_scatter | solution.py:325
  659.9 185.7 %reduce-scatter.9.cloned.1.call-start = ((), (), s32[]{:S(2)}) async-start(), calls=%async_computation.21 | async-start | bytes 2654208 | tf_op jit(solution)/shard_map/reduce_scatter | solution.py:327
  726.4 120.9 %reduce-scatter.11.cloned.1.call-start = ((), (), s32[]{:S(2)}) async-start(), calls=%async_computation.22 | async-start | bytes 2654208 | tf_op jit(solution)/shard_map/reduce_scatter | solution.py:328
  793.5 123.4 %reduce-scatter.15.cloned.1.call-start = ((), (), s32[]{:S(2)}) async-start(), calls=%async_computation.24 | async-start | bytes 10616832 | tf_op jit(solution)/shard_map/reduce_scatter | solution.py:334
  802.5 194.2 %reduce-scatter.17.cloned.1.call-start = ((), (), s32[]{:S(2)}) async-start(), calls=%async_computation.25 | async-start | bytes 10616832 | tf_op jit(solution)/shard_map/reduce_scatter | solution.py:336
  813.2 265.8 %all-reduce.23.cloned.1.call-start = ((), (), s32[]{:S(2)}) async-start(), calls=%async_computation.26 | async-start | bytes 3538944 | tf_op jit(solution)/shard_map/psum | solution.py:358
  825.8 7.0 copy-start.3
  849.0 149.9 %copy-start.10 = (bf16[768,768]{1,0:T(8,128)(2,1)S(1)}, bf16[768,768]{1,0:T(8,128)(2,1)}, u32[]{:S(2)}) copy-start(bf16[768,768]{1,0:T(8,128)(2,1)} %reshape.310) | copy-start | bytes 3538948
  849.0 149.9 %copy-start.34 = (bf16[768,768]{1,0:T(8,128)(2,1)S(1)}, bf16[768,768]{1,0:T(8,128)(2,1)}, u32[]{:S(2)}) copy-start(bf16[768,768]{1,0:T(8,128)(2,1)} %all-gather.10.cloned.1.call-done) | copy-start | bytes 3538948
  1001.3 3.8 copy-start.25
  1001.3 65.9 %copy-start.6 = (f32[768,768]{1,0:T(8,128)S(1)}, f32[768,768]{1,0:T(8,128)}, u32[]{:S(2)}) copy-start(f32[768,768]{1,0:T(8,128)} %copy-done.5) | copy-start | bytes 7077892
  1079.0 4.4 copy-start.15
  1079.0 5.1 copy-start.14
  1079.0 5.9 copy-start.13
  1079.0 6.6 copy-start.12
  (24 other events, 40.0 us)
Sparse Core Ops, SparseCore 0:
  10.0 26.8 all-gather.7
  38.8 24.0 all-gather.11
  64.8 24.0 all-gather.9
  93.2 26.1 all-gather.13
  134.1 41.8 all-gather.15
  312.5 41.8 all-gather.17
  424.5 45.4 reduce-scatter.12
  660.0 43.1 reduce-scatter.6
  726.5 43.1 reduce-scatter.8
  793.6 43.2 reduce-scatter.10
  840.4 76.4 reduce-scatter.14
  920.2 76.4 reduce-scatter.16
  1000.7 78.2 all-reduce.22
where the time goes:
time: 1110 us; the launch traced here: 1090 us
  waiting for transfers between devices  323 us (29%)
  matrix products  266 us (24%)
  blocking collectives  219 us (20%)
  local copies, waits for them, and re-layouts  172 us (15%)
  other arithmetic  68 us (6%)
  starting transfers between devices  27.7 us (2%)
  between operations  16.7 us (2%)
    reduce_scatter x1, waiting for transfers between devices, per_device(): lax.psum_scatter(d_w_down, 'dp', scatter_dimension=0, tiled=True)  77.7 us
    reduce_scatter x1, waiting for transfers between devices, per_device(): lax.psum_scatter(d_w_up, 'dp', scatter_dimension=0, tiled=True)  67.9 us
    unnamed x2, blocking collectives  52.5 us
    all_to_all x1, blocking collectives, per_device(): lax.all_to_all(from_pairs(grad_key_pairs, seqs_here, heads_here), 'seq',...  51.4 us
    all_to_all x1, blocking collectives, per_device(): lax.all_to_all(from_pairs(grad_value_pairs, seqs_here, heads_here), 'seq'...  50.8 us
    all_to_all x1, waiting for transfers between devices, per_device(): lax.all_to_all(from_pairs(grad_query_pairs, seqs_here, heads_here), 'seq'...  45.4 us
    all_gather x1, blocking collectives, per_device(): full_segments = lax.all_gather(segment_ids, 'seq', axis=1, tiled=True)  41.2 us
    dot_general x18, matrix products, masked_scores(): jnp.einsum('qd,kd->qk', query_pair, key_pair, preferred_element_type=jnp....  38.3 us
  transfers between devices with their start and end apart: 19, of which 9 were waited for; matrix products, arithmetic and copies ran while one was open for 41% of the time, Pallas kernels for 0%

commit v1 on v0

--- a/solution.py
+++ b/solution.py
@@ -2,9 +2,22 @@
 import jax.numpy as jnp
 from jax import lax
 from jax.sharding import PartitionSpec as P
+from jax.lax import axis_index, axis_size, ppermute
 
 HD = 64
 EPSILON = 1e-05
+
+
+def advance_shards(chunk, out_dim, frame):
+    y = chunk.shape
+    plain = chunk.reshape(*y[:out_dim], frame, y[out_dim] // frame, *y[out_dim + 1 :])
+    return jnp.moveaxis(plain, out_dim, 0)
+
+
+def bars_run(z, which_dim):
+    opened = list(z.shape[1:])
+    opened[which_dim] *= z.shape[0]
+    return jnp.moveaxis(z, 0, which_dim).reshape(opened)
 
 
 def layer_norm(values, gain, shift):
@@ -118,6 +131,25 @@
     fc2_bias,
     grad_output,
 ):
+
+    def _choose_sample(local_array, group_axis, block_in, frame_in):
+        local_out = axis_index(group_axis)
+        extra = axis_size(group_axis)
+        upper, mid_arr = (extra, local_out)
+        next_value = advance_shards(local_array, block_in, upper)
+        chunks = [next_value[mid_arr]]
+        k0 = 1
+        while k0 < upper:
+            t1 = next_value[(mid_arr + k0) % upper]
+            far_arr = ppermute(
+                t1, group_axis, [(to_i, (to_i + k0) % upper) for to_i in range(upper)]
+            )
+            chunks.append(far_arr)
+            k0 += 1
+        carry_in = jnp.stack(chunks, axis=0)
+        next_value = carry_in[(mid_arr - jnp.arange(upper)) % upper]
+        return bars_run(next_value, frame_in)
+
     seqs_here, positions, model_width = inputs.shape
     token_rows = seqs_here * positions
     (
@@ -262,13 +294,7 @@
         ),
     )
     grad_query_tok, grad_key_tok, grad_value_tok = (
-        lax.all_to_all(
-            from_pairs(grad_query_pairs, seqs_here, heads_here),
-            "seq",
-            split_axis=1,
-            concat_axis=2,
-            tiled=True,
-        ),
+        _choose_sample(from_pairs(grad_query_pairs, seqs_here, heads_here), "seq", 1, 2),
         lax.all_to_all(
             from_pairs(grad_key_pairs, seqs_here, heads_here),
             "seq",

time: 1110 us -> 1090 us (0.982)
  waiting for transfers between devices: 323 us -> 299 us
    all_to_all x1 -> x0, waiting for transfers between devices: 45.4 us -> none  [per_device(): lax.all_to_all(from_pairs(grad_query_pairs, seqs_here, heads_here), 'seq'...]
    ppermute x0 -> x3, waiting for transfers between devices: none -> 16.4 us  [_choose_sample(): ppermute(t1, group_axis, [(to_i, (to_i + k0) % upper) for to_i in range(u...]
    another operation x4 -> x7, local copies, waits for them, and re-layouts: 4.63 us -> 18 us
  transfers between devices with their start and end apart: 19 -> 21, of which waited for: 9 -> 10; matrix products, arithmetic and copies ran while one was open for 41% -> 42% of each run, Pallas kernels for 0% -> 0%
where the time goes in v1:
time: 1090 us; the launch traced here: 1080 us
  waiting for transfers between devices  299 us (27%)
  matrix products  266 us (24%)
  blocking collectives  223 us (20%)
  local copies, waits for them, and re-layouts  176 us (16%)
  other arithmetic  67.8 us (6%)
  starting transfers between devices  27.3 us (3%)
  between operations  16.8 us (2%)
    reduce_scatter x1, waiting for transfers between devices, per_device(): lax.psum_scatter(d_w_down, 'dp', scatter_dimension=0, tiled=True)  77.7 us
    reduce_scatter x1, waiting for transfers between devices, per_device(): lax.psum_scatter(d_w_up, 'dp', scatter_dimension=0, tiled=True)  74 us
    all_to_all x1, blocking collectives, per_device(): lax.all_to_all(from_pairs(grad_key_pairs, seqs_here, heads_here), 'seq',...  54.8 us
    unnamed x2, blocking collectives  52.5 us
    all_to_all x1, blocking collectives, per_device(): lax.all_to_all(from_pairs(grad_value_pairs, seqs_here, heads_here), 'seq'...  50.8 us
    all_gather x1, blocking collectives, per_device(): full_segments = lax.all_gather(segment_ids, 'seq', axis=1, tiled=True)  41.2 us
    dot_general x18, matrix products, masked_scores(): jnp.einsum('qd,kd->qk', query_pair, key_pair, preferred_element_type=jnp....  38.4 us
    dot_general x9, matrix products, attend_forward(): jnp.dot(probs, value_pair, preferred_element_type=jnp.float32)  37.7 us
  transfers between devices with their start and end apart: 21, of which 10 were waited for; matrix products, arithmetic and copies ran while one was open for 42% of the time, Pallas kernels for 0%

profile of v1, /device:TPU:0, one launch (start us, length us, event | category | flops | bytes accessed | tf_op | source)
XLA Modules:
  0.0 1076.5 jit_solution(9071887962067162375)
XLA Ops:
  15.2 26.3 %all-reduce.18 = (bf16[768]{0:T(1024)(128)(2,1)S(1)}, bf16[768]{0:T(1024)(128)(2,1)S(1)}, bf16[768]{0:T(1024)(128)(2,1)S(1)}, bf16[768]{0:T(1024)(128)(2,1)S(1)}...) all-reduce(bf16[768]{0:T(1024)(128)(2,1)S(1)} %dynamic-update-slice, ...), channel_id=1, replica_groups=mesh['dp'=8,'seq'=4] {'dp'}, use_global_device_ids=true, to_apply=%add.1 | all-reduce | flops 6144 | bytes 24576
  47.7 5.0 all-to-all-start
  53.4 9.6 all-gather.12.cloned.1.call-done
  70.3 16.2 %all-to-all-done = bf16[3,256,768]{1,0,2:T(4,128)(2,1)S(1)} async-done(((bf16[3,256,768]{1,0,2:T(4,128)(2,1)}), bf16[3,256,768]{1,0,2:T(4,128)(2,1)S(1)}, u32[]{:S(2)}, u32[]{:S(2)}) %all-to-all-start) | async-done | bytes 1179680 | tf_op jit(solution)/shard_map/all_to_all | solution.py:202
  86.5 4.4 all-to-all-start.2
  98.7 28.6 %all-to-all-done.2 = bf16[3,256,768]{1,0,2:T(4,128)(2,1)} async-done(((bf16[3,256,768]{1,0,2:T(4,128)(2,1)}), bf16[3,256,768]{1,0,2:T(4,128)(2,1)}, u32[]{:S(2)}, u32[]{:S(2)}) %all-to-all-start.2) | async-done | bytes 1179680 | tf_op jit(solution)/shard_map/all_to_all | solution.py:216
  127.3 4.3 all-to-all-start.1
  132.3 41.2 %all_gather.56 = s32[3,1024]{1,0:T(4,128)S(1)} all-gather(s32[3,256]{1,0:T(4,128)S(1)} %copy-done.31), channel_id=1, replica_groups=mesh['dp'=8,'seq'=4] {'seq'}, dimensions={1}, use_global_device_ids=true | all-gather | bytes 15360 | tf_op jit(solution)/shard_map/all_gather | solution.py:188
  202.0 99.5 %while.26 = (s32[]{:T(128)}, bf16[9,1024,64]{1,2,0:T(8,128)(2,1)}, f32[9,1024]{1,0:T(8,128)}, s32[9,1024]{1,0:T(8,128)}, bf16[9,1024,64]{2,1,0:T(8,128)(2,1)S(1)...) while((s32[]{:T(128)}, bf16[9,1024,64]{1,2,0:T(8,128)(2,1)}, ...), condition=%wide.region_5.6_spmd, body=%wide.region_2.5_spmd.sunk | while | flops 284228608 | bytes 30349440 | solution.py:229
  208.9 4.2 fusion.158
  220.0 4.2 fusion.158
  231.0 4.2 fusion.158
  242.1 4.2 fusion.158
  253.1 4.2 fusion.158
  264.2 4.2 fusion.158
  275.2 4.2 fusion.158
  286.3 4.2 fusion.158
  297.3 4.2 fusion.158
  301.5 4.3 copy.111
  305.8 4.6 all-to-all-start.3
  311.7 10.1 all-gather
  322.4 33.6 %all-to-all-done.3 = bf16[3,1024,192]{2,0,1:T(4,128)(2,1)} async-done(((bf16[3,1024,192]{2,0,1:T(4,128)(2,1)}), bf16[3,1024,192]{2,0,1:T(4,128)(2,1)}, u32[]{:S(2)}, u32[]{:S(2)}) %all-to-all-start.3) | async-done | bytes 1179680 | tf_op jit(solution)/shard_map/all_to_all | solution.py:233
  364.5 27.3 %fusion.56 = (bf16[768,3072]{1,0:T(8,128)(2,1)}, f32[768,3072]{1,0:T(8,128)}) fusion(f32[3072]{0:T(1024)} %bitcast.299, bf16[768,3072]{1,0:T(8,128)(2,1)} %all-gather.16.cloned.1.call-done, f32[768,768]{1,0:T(8,128)S(1)} %get-tuple-element.269, f32[768]{0:T(1024)S(1)} %convert_element_type.227, f32[768]{0:T(1024)S(1)} %convert_element_type.226, ...), kind=kOutput, calls=%fused_computation.65 | convolution fusion | flops 3782541312 | bytes 21258240 | tf_op jit(solution)/shard_map/dot_general | solution.py:245
  391.8 11.6 %convert_reduce_fusion = (f32[3072]{0:T(1024)}, bf16[768,3072]{1,0:T(8,128)(2,1)S(1)}) fusion(f32[768,3072]{1,0:T(8,128)} %get-tuple-element.271, f32[3072]{0:T(1024)} %bitcast.300, bf16[768,768]{1,0:T(8,128)(2,1)} %bitcast.266, bf16[3072,768]{1,0:T(8,128)(2,1)} %all-gather.18.cloned.1.call-done), kind=kOutput, calls=%fused_computation.72 | convolution fusion | flops 3654546432 | bytes 20078592 | tf_op jit(solution)/shard_map/dot_general | solution.py:53
  403.4 4.8 multiply_reduce_fusion.1
  415.7 4.4 all-to-all-start.4
  420.7 4.6 fusion.92
  425.3 31.3 %all-to-all-done.4 = bf16[3,256,768]{1,0,2:T(4,128)(2,1)} async-done(((bf16[3,256,768]{1,0,2:T(4,128)(2,1)}), bf16[3,256,768]{1,0,2:T(4,128)(2,1)}, u32[]{:S(2)}, u32[]{:S(2)}) %all-to-all-start.4) | async-done | bytes 1179680 | tf_op jit(solution)/shard_map/all_to_all | solution.py:284
  467.3 124.2 %while.27 = (s32[]{:T(128)}, bf16[9,1024,64]{1,2,0:T(8,128)(2,1)}, bf16[9,1024,64]{1,2,0:T(8,128)(2,1)}, bf16[9,1024,64]{1,2,0:T(8,128)(2,1)}, s32[9,1024]{1,0:T...) while((s32[]{:T(128)}, bf16[9,1024,64]{1,2,0:T(8,128)(2,1)}, ...), condition=%wide.region_12.13_spmd, body=%wide.region_10.12_spmd.sunk | while | flops 681901056 | bytes 33465460 | solution.py:285
  595.0 5.9 constant_dynamic-slice_fusion.6
  607.3 5.6 collective-permute-done
  612.9 10.8 collective-permute-done.1
  635.4 4.1 fusion.101
  639.6 4.3 copy.122
  643.9 54.8 %all_to_all.105 = bf16[3,1024,192]{2,0,1:T(4,128)(2,1)S(1)} all-to-all(bf16[3,1024,192]{2,0,1:T(4,128)(2,1)} %copy.122), channel_id=1, replica_groups=mesh['dp'=8,'seq'=4] {'seq'}, dimensions={1} | all-to-all | bytes 2359296 | tf_op jit(solution)/shard_map/all_to_all | solution.py:298
  705.4 4.2 fusion.102
  709.7 4.1 copy.125
  713.7 50.8 %all_to_all.106 = bf16[3,1024,192]{2,0,1:T(4,128)(2,1)S(1)} all-to-all(bf16[3,1024,192]{2,0,1:T(4,128)(2,1)} %copy.125), channel_id=1, replica_groups=mesh['dp'=8,'seq'=4] {'seq'}, dimensions={1} | all-to-all | bytes 2359296 | tf_op jit(solution)/shard_map/all_to_all | solution.py:305
  772.6 4.1 fusion.103
  776.8 9.0 fusion.95
  786.1 10.5 fusion.104
  800.3 8.7 add_convert_fusion
  809.9 4.3 fusion.99
  826.3 74.0 %reduce-scatter.15.cloned.1.call-done = f32[96,3072]{1,0:T(8,128)} async-done(((f32[768,3072]{1,0:T(8,128)}), f32[96,3072]{1,0:T(8,128)}) %reduce-scatter.15.cloned.1.call-update) | async-done | bytes 1179664 | tf_op jit(solution)/shard_map/reduce_scatter | solution.py:360
  902.4 77.7 %reduce-scatter.17.cloned.1.call-done = f32[384,768]{1,0:T(8,128)} async-done(((f32[3072,768]{1,0:T(8,128)}), f32[384,768]{1,0:T(8,128)}) %reduce-scatter.17.cloned.1.call-update) | async-done | bytes 1179664 | tf_op jit(solution)/shard_map/reduce_scatter | solution.py:362
  988.5 26.3 %all-reduce.17 = (bf16[768]{0:T(1024)(128)(2,1)}, bf16[768]{0:T(1024)(128)(2,1)}, bf16[768]{0:T(1024)(128)(2,1)}, bf16[768]{0:T(1024)(128)(2,1)}, bf16[768]{0:T(...) all-reduce(f32[768]{0:T(1024)} %get-tuple-element.184, ...), channel_id=2, replica_groups=mesh['dp'=8,'seq'=4] {'dp'}, use_global_device_ids=true, to_apply=%region_16.17.clone | all-reduce | flops 9216 | bytes 55296
  1025.5 13.1 %all-reduce.19 = (bf16[96]{0:T(256)(128)(2,1)}, bf16[96]{0:T(256)(128)(2,1)}, bf16[96]{0:T(256)(128)(2,1)}, bf16[96]{0:T(256)(128)(2,1)}, bf16[96]{0:T(256)(128)...) all-reduce(bf16[96]{0:T(256)(128)(2,1)} %dynamic-slice.63, ...), channel_id=1, replica_groups=mesh['dp'=8,'seq'=4] {'seq'}, use_global_device_ids=true, to_apply=%region_17.18 | all-reduce | flops 1152 | bytes 4608 | tf_op jit(solution)/shard_map/psum | solution.py:382
  1054.0 8.4 all-reduce.23.cloned.1.call-done
  (405 shorter events, 368.9 us)
Async XLA Ops:
  7.2 4.9 copy-start.36
  7.2 34.9 %copy-start.1 = (bf16[3,256,768]{2,1,0:T(8,128)(2,1)S(1)}, bf16[3,256,768]{2,1,0:T(8,128)(2,1)}, u32[]{:S(2)}) copy-start(bf16[3,256,768]{2,1,0:T(8,128)(2,1)} %param.22) | copy-start | bytes 3538948
  7.2 6.1 copy-start.42
  7.2 6.4 copy-start.43
  7.2 6.6 copy-start.44
  7.2 6.8 copy-start.45
  7.3 7.0 copy-start.46
  7.3 7.3 copy-start.47
  7.3 7.5 copy-start.48
  7.3 7.7 copy-start.49
  7.3 35.4 %all-gather.8.cloned.1.call-start = ((), (), s32[]{:S(2)}) async-start(), calls=%async_computation.13 | async-start | bytes 1327104 | tf_op jit(solution)/shard_map/all_gather | solution.py:174
  8.0 54.9 %all-gather.12.cloned.1.call-start = ((), (), s32[]{:S(2)}) async-start(), calls=%async_computation.15 | async-start | bytes 1327104 | tf_op jit(solution)/shard_map/all_gather | solution.py:177
  10.3 31.3 %copy-start.20 = (f32[3,256]{1,0:T(4,128)}, f32[3,256]{1,0:T(4,128)S(1)}, u32[]{:S(2)}) copy-start(f32[3,256]{1,0:T(4,128)S(1)} %broadcast_multiply_fusion.5) | copy-start | bytes 9220
  12.1 30.6 %copy-start.22 = (f32[768]{0:T(1024)}, f32[768]{0:T(1024)S(1)}, u32[]{:S(2)}) copy-start(f32[768]{0:T(1024)S(1)} %div.35) | copy-start | bytes 9220
  47.7 38.8 %all-to-all-start = ((bf16[3,256,768]{1,0,2:T(4,128)(2,1)}), bf16[3,256,768]{1,0,2:T(4,128)(2,1)S(1)}, u32[]{:S(2)}, u32[]{:S(2)}) async-start(bf16[3,256,768]{1,0,2:T(4,128)(2,1)} %copy.99), calls=%async_computation | async-start | bytes 3145728 | tf_op jit(solution)/shard_map/all_to_all | solution.py:202
  52.6 38.8 %all-gather.10.cloned.1.call-start = ((), (), s32[]{:S(2)}) async-start(), calls=%async_computation.14 | async-start | bytes 1327104 | tf_op jit(solution)/shard_map/all_gather | solution.py:176
  86.5 40.9 %all-to-all-start.2 = ((bf16[3,256,768]{1,0,2:T(4,128)(2,1)}), bf16[3,256,768]{1,0,2:T(4,128)(2,1)}, u32[]{:S(2)}, u32[]{:S(2)}) async-start(bf16[3,256,768]{1,0,2:T(4,128)(2,1)} %copy.105), calls=%async_computation.2 | async-start | bytes 3145728 | tf_op jit(solution)/shard_map/all_to_all | solution.py:216
  90.8 270.4 %all-gather.14.cloned.1.call-start = ((), (), s32[]{:S(2)}) async-start(), calls=%async_computation.16 | async-start | bytes 1327104 | tf_op jit(solution)/shard_map/all_gather | solution.py:179
  98.7 33.6 %copy-start.31 = (s32[3,256]{1,0:T(4,128)S(1)}, s32[3,256]{1,0:T(4,128)}, u32[]{:S(2)}) copy-start(s32[3,256]{1,0:T(4,128)} %param.23) | copy-start | bytes 9220
  127.3 62.9 %all-to-all-start.1 = ((bf16[3,256,768]{1,0,2:T(4,128)(2,1)}), bf16[3,256,768]{1,0,2:T(4,128)(2,1)}, u32[]{:S(2)}, u32[]{:S(2)}) async-start(bf16[3,256,768]{1,0,2:T(4,128)(2,1)} %copy.102), calls=%async_computation.1 | async-start | bytes 3145728 | tf_op jit(solution)/shard_map/all_to_all | solution.py:209
  131.7 232.8 %all-gather.16.cloned.1.call-start = ((), (), s32[]{:S(2)}) async-start(), calls=%async_computation.17 | async-start | bytes 5308416 | tf_op jit(solution)/shard_map/all_gather | solution.py:183
  305.8 5.2 copy-start.35
  305.8 5.2 copy-start.34
  305.8 5.2 copy-start.33
  305.8 50.1 %all-to-all-start.3 = ((bf16[3,1024,192]{2,0,1:T(4,128)(2,1)}), bf16[3,1024,192]{2,0,1:T(4,128)(2,1)}, u32[]{:S(2)}, u32[]{:S(2)}) async-start(bf16[3,1024,192]{2,0,1:T(4,128)(2,1)} %copy.111), calls=%async_computation.3 | async-start | bytes 4194304 | tf_op jit(solution)/shard_map/all_to_all | solution.py:233
  310.4 81.4 %all-gather.18.cloned.1.call-start = ((), (), s32[]{:S(2)}) async-start(), calls=%async_computation.18 | async-start | bytes 5308416 | tf_op jit(solution)/shard_map/all_gather | solution.py:185
  391.8 11.6 %copy-start.38 = (bf16[768,3072]{1,0:T(8,128)(2,1)S(1)}, bf16[768,3072]{1,0:T(8,128)(2,1)}, u32[]{:S(2)}) copy-start(bf16[768,3072]{1,0:T(8,128)(2,1)} %all-gather.16.cloned.1.call-done) | copy-start | bytes 14155780
  403.4 4.8 copy-start.9
  403.4 4.8 copy-start.8
  415.7 40.9 %all-to-all-start.4 = ((bf16[3,256,768]{1,0,2:T(4,128)(2,1)}), bf16[3,256,768]{1,0,2:T(4,128)(2,1)}, u32[]{:S(2)}, u32[]{:S(2)}) async-start(bf16[3,256,768]{1,0,2:T(4,128)(2,1)} %copy.114), calls=%async_computation.4 | async-start | bytes 3145728 | tf_op jit(solution)/shard_map/all_to_all | solution.py:284
  420.1 399.7 %reduce-scatter.13.cloned.1.call-start = ((), (), s32[]{:S(2)}) async-start(), calls=%async_computation.22 | async-start | bytes 2654208 | tf_op jit(solution)/shard_map/reduce_scatter | solution.py:356
  425.3 396.1 %reduce-scatter.7.cloned.1.call-start = ((), (), s32[]{:S(2)}) async-start(), calls=%async_computation.19 | async-start | bytes 2654208 | tf_op jit(solution)/shard_map/reduce_scatter | solution.py:351
  600.9 4.8 copy-start.18
  601.0 11.9 %collective-permute-start = (bf16[3,256,192]{1,2,0:T(8,128)(2,1)S(1)}, bf16[3,256,192]{1,2,0:T(8,128)(2,1)S(1)}, u32[]{:S(2)}, u32[]{:S(2)}) collective-permute-start(bf16[3,256,192]{1,2,0:T(8,128)(2,1)S(1)} %bitcast.296), channel_id=1, source_target_pairs={{0,1},{1,2},{2,3},{3,0},{4,5},{5,6},{6,7},{7,4},{8,9},{9,10},{10,1... | collective-permute-start | bytes 884744 | tf_op jit(solution)/shard_map/ppermute | solution.py:144
  601.1 22.5 %collective-permute-start.1 = (bf16[3,256,192]{1,2,0:T(8,128)(2,1)S(1)}, bf16[3,256,192]{1,2,0:T(8,128)(2,1)S(1)}, u32[]{:S(2)}, u32[]{:S(2)}) collective-permute-start(bf16[3,256,192]{1,2,0:T(8,128)(2,1)S(1)} %bitcast.297), channel_id=1, source_target_pairs={{0,2},{1,3},{2,0},{3,1},{4,6},{5,7},{6,4},{7,5},{8,10},{9,11},{10,... | collective-permute-start | bytes 884744 | tf_op jit(solution)/shard_map/ppermute | solution.py:144
  603.2 20.4 %collective-permute-start.2 = (bf16[3,256,192]{1,2,0:T(8,128)(2,1)S(1)}, bf16[3,256,192]{1,2,0:T(8,128)(2,1)S(1)}, u32[]{:S(2)}, u32[]{:S(2)}) collective-permute-start(bf16[3,256,192]{1,2,0:T(8,128)(2,1)S(1)} %bitcast.298), channel_id=1, source_target_pairs={{0,3},{1,0},{2,1},{3,2},{4,7},{5,4},{6,5},{7,6},{8,11},{9,8},{10,9... | collective-permute-start | bytes 884744 | tf_op jit(solution)/shard_map/ppermute | solution.py:144
  639.6 183.4 %reduce-scatter.9.cloned.1.call-start = ((), (), s32[]{:S(2)}) async-start(), calls=%async_computation.20 | async-start | bytes 2654208 | tf_op jit(solution)/shard_map/reduce_scatter | solution.py:353
  709.6 115.0 %reduce-scatter.11.cloned.1.call-start = ((), (), s32[]{:S(2)}) async-start(), calls=%async_computation.21 | async-start | bytes 2654208 | tf_op jit(solution)/shard_map/reduce_scatter | solution.py:354
  776.8 123.5 %reduce-scatter.15.cloned.1.call-start = ((), (), s32[]{:S(2)}) async-start(), calls=%async_computation.23 | async-start | bytes 10616832 | tf_op jit(solution)/shard_map/reduce_scatter | solution.py:360
  785.8 194.3 %reduce-scatter.17.cloned.1.call-start = ((), (), s32[]{:S(2)}) async-start(), calls=%async_computation.24 | async-start | bytes 10616832 | tf_op jit(solution)/shard_map/reduce_scatter | solution.py:362
  796.6 265.7 %all-reduce.23.cloned.1.call-start = ((), (), s32[]{:S(2)}) async-start(), calls=%async_computation.25 | async-start | bytes 3538944 | tf_op jit(solution)/shard_map/psum | solution.py:384
  800.3 8.7 copy-start.4
  826.3 156.0 %copy-start.11 = (bf16[768,768]{1,0:T(8,128)(2,1)S(1)}, bf16[768,768]{1,0:T(8,128)(2,1)}, u32[]{:S(2)}) copy-start(bf16[768,768]{1,0:T(8,128)(2,1)} %reshape.357) | copy-start | bytes 3538948
  826.3 156.0 %copy-start.40 = (bf16[768,768]{1,0:T(8,128)(2,1)S(1)}, bf16[768,768]{1,0:T(8,128)(2,1)}, u32[]{:S(2)}) copy-start(bf16[768,768]{1,0:T(8,128)(2,1)} %all-gather.10.cloned.1.call-done) | copy-start | bytes 3538948
  984.7 65.8 %copy-start.7 = (f32[768,768]{1,0:T(8,128)S(1)}, f32[768,768]{1,0:T(8,128)}, u32[]{:S(2)}) copy-start(f32[768,768]{1,0:T(8,128)} %copy-done.6) | copy-start | bytes 7077892
  1062.3 5.1 copy-start.15
  1062.4 5.9 copy-start.14
  1062.4 6.6 copy-start.13
  (32 other events, 75.5 us)
Sparse Core Ops, SparseCore 0:
  10.0 26.8 all-gather.7
  38.8 24.0 all-gather.11
  64.8 24.0 all-gather.9
  93.2 26.1 all-gather.13
  134.1 41.8 all-gather.15
  312.8 41.8 all-gather.17
  425.4 45.4 reduce-scatter.12
  639.7 47.7 reduce-scatter.6
  709.7 43.3 reduce-scatter.8
  776.9 43.2 reduce-scatter.10
  823.7 76.4 reduce-scatter.14
  903.6 76.4 reduce-scatter.16
  984.1 78.1 all-reduce.22
